TPU v7x, 32 devices: a whole 2x2x4 slice. The times are simulated.
32 devices in a mesh: row: 4 (over z), col: 4 (over y, x), depth: 2 (over core).
Axes of the slice: x: 2, y: 2, z: 4, core: 2. Of those that a mesh axis runs over, the one named last changes fastest.
Arguments:
- tiles: float32 [4, 4, 96, 256, 256], P('row', 'col', 'depth'), as said below
- tile_rows: int32 [4, 4, 96], P('row', 'col', 'depth'), may hold values from 0 to 127, as said below
- tile_cols: int32 [4, 4, 96], P('row', 'col', 'depth'), may hold values from 0 to 127
- tile_count: int32 [4, 4, 2], P('row', 'col', 'depth'), may hold values from 16 to 48, as said below
Outputs:
- row_scale: float32 [131072], P('row')
- col_scale: float32 [131072], P('col')
- scaled_tiles: float32 [4, 4, 96, 256, 256], P('row', 'col', 'depth')
Inputs may be any that keep to these rules, and one draw needn't show every extreme that they name: `tile_rows`: every block row and every block column of the matrix holds a live tile; no block is listed twice among the live tiles of the two depth lists of one row and col index. `tile_count`: some device's list is full in every draw. `tiles`: entries in empty slots are ignored.
All inputs are finite; a program needn't handle non-finite values.
Results may differ from a plain program's by a relative error of at most 0.0001.
Values sent between devices are 32-bit elements; how exact they have to be, the bound alone decides.
A program may use at most 128 MiB of HBM per device.

v0:
```python
import math
import jax
import jax.numpy as jnp
from jax import lax
from jax.sharding import PartitionSpec as P

RB_DEV = 128
ANCHORS = 16
SWEEPS = 4
EPS = 1e-06


def shards(tiles, tile_rows, tile_cols, tile_count):
    all_values = tiles[0, 0]
    row_index = tile_rows[0, 0]
    col_index = tile_cols[0, 0]
    live_count = tile_count[0, 0, 0]
    slot_count = all_values.shape[0]
    tile_size = all_values.shape[1]
    col_blocks = lax.axis_size("row") * lax.axis_size("depth") * ANCHORS
    group_size = math.gcd(slot_count, 8)
    block_count = (live_count + group_size - 1) // group_size
    row_ids = jnp.arange(RB_DEV, dtype=jnp.int32)
    col_ids = jnp.arange(col_blocks, dtype=jnp.int32)

    def partials(row_now, col_now, summed):

        def step_block(position, carry):
            row_acc, col_acc = carry
            first_slot = position * group_size
            block_values = lax.dynamic_slice_in_dim(all_values, first_slot, group_size, 0)
            block_rows = lax.dynamic_slice_in_dim(row_index, first_slot, group_size, 0)
            block_cols = lax.dynamic_slice_in_dim(col_index, first_slot, group_size, 0)
            live_mask = first_slot + jnp.arange(group_size, dtype=jnp.int32) < live_count
            scaled = (
                block_values * row_now[block_rows][:, :, None] * col_now[block_cols][:, None, :]
            )
            magnitude = jnp.where(live_mask[:, None, None], jnp.abs(scaled), jnp.float32(0.0))
            row_hit = row_ids[:, None] == block_rows[None, :]
            col_hit = col_ids[:, None] == block_cols[None, :]
            if summed:
                row_acc = row_acc + jnp.dot(
                    row_hit.astype(jnp.float32),
                    magnitude.sum(axis=2),
                    precision=lax.Precision.HIGHEST,
                )
                col_acc = col_acc + jnp.dot(
                    col_hit.astype(jnp.float32),
                    magnitude.sum(axis=1),
                    precision=lax.Precision.HIGHEST,
                )
            else:
                row_acc = jnp.maximum(
                    row_acc,
                    jnp.where(
                        row_hit[:, :, None], magnitude.max(axis=2)[None], jnp.float32(0.0)
                    ).max(axis=1),
                )
                col_acc = jnp.maximum(
                    col_acc,
                    jnp.where(
                        col_hit[:, :, None], magnitude.max(axis=1)[None], jnp.float32(0.0)
                    ).max(axis=1),
                )
            return (row_acc, col_acc)

        initial = (
            jnp.zeros((RB_DEV, tile_size), jnp.float32),
            jnp.zeros((col_blocks, tile_size), jnp.float32),
        )
        return lax.fori_loop(0, block_count, step_block, initial)

    row_factor = jnp.ones((RB_DEV, tile_size), jnp.float32)
    col_factor = jnp.ones((col_blocks, tile_size), jnp.float32)
    for sweep_index in range(SWEEPS):
        row_part, col_part = partials(row_factor, col_factor, False)
        row_pair, col_pair = lax.pmax((row_part, col_part), "depth")
        row_peak = lax.pmax(row_pair, "col")
        col_peak = lax.pmax(col_pair, "row")
        row_factor = row_factor * lax.rsqrt(row_peak + EPS)
        col_factor = col_factor * lax.rsqrt(col_peak + EPS)
    row_part, col_part = partials(row_factor, col_factor, True)
    row_mass = lax.psum(row_part, ("col", "depth"))
    col_mass = lax.psum(col_part, ("row", "depth"))
    row_factor = row_factor * lax.rsqrt(row_mass + EPS)
    col_factor = col_factor * lax.rsqrt(col_mass + EPS)
    live_all = jnp.arange(slot_count, dtype=jnp.int32) < live_count
    scaled_all = all_values * row_factor[row_index][:, :, None] * col_factor[col_index][:, None, :]
    scaled_all = jnp.where(live_all[:, None, None], scaled_all, jnp.float32(0.0))
    return (row_factor.reshape(-1), col_factor.reshape(-1), scaled_all[None, None])


def solution(mesh):
    in_specs = (
        P("row", "col", "depth", None, None),
        P("row", "col", "depth"),
        P("row", "col", "depth"),
        P("row", "col", "depth"),
    )
    out_specs = (P("row"), P("col"), P("row", "col", "depth", None, None))
    return jax.shard_map(shards, mesh=mesh, in_specs=in_specs, out_specs=out_specs, check_vma=False)
```

profile of v0, /device:TPU:0, one launch (start us, length us, event | category | flops | bytes accessed | tf_op | source)
XLA Modules:
  0.0 722.1 jit_solution(14367923665303358585)
XLA Ops:
  7.9 17.5 %while.75 = (s32[]{:T(128)}, f32[128,256]{1,0:T(8,128)S(1)}, f32[128,256]{1,0:T(8,128)S(1)}, s32[]{:T(128)}, s32[48]{0:T(128)}, /*index=5*/s32[]{:T(128)}, f32[4...) while((s32[]{:T(128)}, f32[128,256]{1,0:T(8,128)S(1)}, ...), condition=%wide.region_5.6_spmd.clone.clone, body=%wide.region_0.5_spmd.clone.clone.sunk | while | flops 4194374 | bytes 3371599 | solution.py:71
  10.6 2.3 fusion.33
  14.4 0.8 compare_select_fusion.17
  16.4 2.3 fusion.33
  20.3 0.8 compare_select_fusion.17
  22.3 2.3 fusion.33
  26.2 37.1 %all-reduce.45.cloned.1.call-done = (f32[128,256]{1,0:T(8,128)}, f32[128,256]{1,0:T(8,128)}) async-done(((f32[128,256]{1,0:T(8,128)}, f32[128,256]{1,0:T(8,128)}), (f32[128,256]{1,0:T(8,128)}, f32[128,256]{1,0:T(8,128)})) %all-reduce.45.cloned.1.call-update) | async-done | bytes 262160 | tf_op jit(solution)/shard_map/pmax | solution.py:77
  64.2 37.4 %all-reduce.21.cloned.1.call-done = f32[128,256]{1,0:T(8,128)} async-done(((f32[128,256]{1,0:T(8,128)}), f32[128,256]{1,0:T(8,128)}) %all-reduce.21.cloned.1.call-update) | async-done | bytes 131088 | tf_op jit(solution)/shard_map/pmax | solution.py:79
  101.6 0.9 add_rsqrt_fusion
  102.5 44.0 %all-reduce.19.cloned.1.call-done = f32[128,256]{1,0:T(8,128)} async-done(((f32[128,256]{1,0:T(8,128)}), f32[128,256]{1,0:T(8,128)}) %all-reduce.19.cloned.1.call-update) | async-done | bytes 131088 | tf_op jit(solution)/shard_map/pmax | solution.py:78
  146.5 0.9 add_rsqrt_fusion.1
  147.5 17.5 %while.76 = (s32[]{:T(128)}, f32[128,256]{1,0:T(8,128)S(1)}, f32[128,256]{1,0:T(8,128)S(1)}, s32[]{:T(128)}, s32[48]{0:T(128)}, /*index=5*/s32[]{:T(128)}, f32[4...) while((s32[]{:T(128)}, f32[128,256]{1,0:T(8,128)S(1)}, ...), condition=%wide.region_15.16_spmd.clone.clone, body=%wide.region_10.15_spmd.clone.clone.sunk | while | flops 4194374 | bytes 3240531 | solution.py:71
  148.3 0.8 compare_select_fusion.18
  150.2 2.3 fusion.34
  156.0 2.3 fusion.34
  161.8 2.3 fusion.34
  165.8 34.9 %all-reduce.43.cloned.1.call-done = (f32[128,256]{1,0:T(8,128)}, f32[128,256]{1,0:T(8,128)}) async-done(((f32[128,256]{1,0:T(8,128)}, f32[128,256]{1,0:T(8,128)}), (f32[128,256]{1,0:T(8,128)}, f32[128,256]{1,0:T(8,128)})) %all-reduce.43.cloned.1.call-update) | async-done | bytes 262160 | tf_op jit(solution)/shard_map/pmax | solution.py:77
  201.4 45.6 %all-reduce.23.cloned.1.call-done = f32[128,256]{1,0:T(8,128)} async-done(((f32[128,256]{1,0:T(8,128)}), f32[128,256]{1,0:T(8,128)}) %all-reduce.23.cloned.1.call-update) | async-done | bytes 131088 | tf_op jit(solution)/shard_map/pmax | solution.py:78
  247.0 0.9 rsqrt_multiply_fusion.7
  248.0 35.9 %all-reduce.25.cloned.1.call-done = f32[128,256]{1,0:T(8,128)} async-done(((f32[128,256]{1,0:T(8,128)}), f32[128,256]{1,0:T(8,128)}) %all-reduce.25.cloned.1.call-update) | async-done | bytes 131088 | tf_op jit(solution)/shard_map/pmax | solution.py:79
  283.9 0.9 rsqrt_multiply_fusion.6
  284.9 17.5 %while.77 = (s32[]{:T(128)}, f32[128,256]{1,0:T(8,128)S(1)}, f32[128,256]{1,0:T(8,128)S(1)}, s32[]{:T(128)}, s32[48]{0:T(128)}, /*index=5*/s32[]{:T(128)}, f32[4...) while((s32[]{:T(128)}, f32[128,256]{1,0:T(8,128)S(1)}, ...), condition=%wide.region_25.26_spmd.clone.clone, body=%wide.region_20.25_spmd.clone.clone.sunk | while | flops 4194374 | bytes 3240531 | solution.py:71
  287.5 2.3 fusion.35
  293.3 2.3 fusion.35
  299.1 2.3 fusion.35
  303.2 34.9 %all-reduce.41.cloned.1.call-done = (f32[128,256]{1,0:T(8,128)}, f32[128,256]{1,0:T(8,128)}) async-done(((f32[128,256]{1,0:T(8,128)}, f32[128,256]{1,0:T(8,128)}), (f32[128,256]{1,0:T(8,128)}, f32[128,256]{1,0:T(8,128)})) %all-reduce.41.cloned.1.call-update) | async-done | bytes 262160 | tf_op jit(solution)/shard_map/pmax | solution.py:77
  338.8 45.6 %all-reduce.27.cloned.1.call-done = f32[128,256]{1,0:T(8,128)} async-done(((f32[128,256]{1,0:T(8,128)}), f32[128,256]{1,0:T(8,128)}) %all-reduce.27.cloned.1.call-update) | async-done | bytes 131088 | tf_op jit(solution)/shard_map/pmax | solution.py:78
  384.5 0.9 rsqrt_multiply_fusion.5
  385.4 36.1 %all-reduce.29.cloned.1.call-done = f32[128,256]{1,0:T(8,128)} async-done(((f32[128,256]{1,0:T(8,128)}), f32[128,256]{1,0:T(8,128)}) %all-reduce.29.cloned.1.call-update) | async-done | bytes 131088 | tf_op jit(solution)/shard_map/pmax | solution.py:79
  421.5 0.9 rsqrt_multiply_fusion.4
  422.5 17.5 %while.78 = (s32[]{:T(128)}, f32[128,256]{1,0:T(8,128)S(1)}, f32[128,256]{1,0:T(8,128)S(1)}, s32[]{:T(128)}, s32[48]{0:T(128)}, /*index=5*/s32[]{:T(128)}, f32[4...) while((s32[]{:T(128)}, f32[128,256]{1,0:T(8,128)S(1)}, ...), condition=%wide.region_35.36_spmd.clone.clone, body=%wide.region_30.35_spmd.clone.clone.sunk | while | flops 4194374 | bytes 3240531 | solution.py:71
  425.0 2.3 fusion.36
  430.9 2.3 fusion.36
  436.7 2.3 fusion.36
  442.0 33.5 %all-reduce.39.cloned.1.call-done = (f32[128,256]{1,0:T(8,128)}, f32[128,256]{1,0:T(8,128)}) async-done(((f32[128,256]{1,0:T(8,128)}, f32[128,256]{1,0:T(8,128)}), (f32[128,256]{1,0:T(8,128)}, f32[128,256]{1,0:T(8,128)})) %all-reduce.39.cloned.1.call-update) | async-done | bytes 262160 | tf_op jit(solution)/shard_map/pmax | solution.py:77
  476.2 45.8 %all-reduce.31.cloned.1.call-done = f32[128,256]{1,0:T(8,128)} async-done(((f32[128,256]{1,0:T(8,128)}), f32[128,256]{1,0:T(8,128)}) %all-reduce.31.cloned.1.call-update) | async-done | bytes 131088 | tf_op jit(solution)/shard_map/pmax | solution.py:78
  522.0 0.9 rsqrt_multiply_fusion.3
  522.9 35.9 %all-reduce.33.cloned.1.call-done = f32[128,256]{1,0:T(8,128)} async-done(((f32[128,256]{1,0:T(8,128)}), f32[128,256]{1,0:T(8,128)}) %all-reduce.33.cloned.1.call-update) | async-done | bytes 131088 | tf_op jit(solution)/shard_map/pmax | solution.py:79
  558.9 0.9 rsqrt_multiply_fusion.2
  559.9 16.1 %while.79 = (s32[]{:T(128)}, f32[128,256]{1,0:T(8,128)S(1)}, f32[128,256]{1,0:T(8,128)S(1)}, s32[]{:T(128)}, s32[48]{0:T(128)}, /*index=5*/s32[]{:T(128)}, f32[4...) while((s32[]{:T(128)}, f32[128,256]{1,0:T(8,128)S(1)}, ...), condition=%wide.region_43.44_spmd.clone.clone, body=%wide.region_40.43_spmd.clone.clone.sunk | while | flops 9502790 | bytes 2712147 | solution.py:71
  562.5 2.3 fusion.39
  567.8 2.3 fusion.39
  573.2 2.3 fusion.39
  577.3 68.2 %all-reduce.35.cloned.1.call-done = f32[128,256]{1,0:T(8,128)} async-done(((f32[128,256]{1,0:T(8,128)}), f32[128,256]{1,0:T(8,128)}) %all-reduce.35.cloned.1.call-update) | async-done | bytes 131088 | tf_op jit(solution)/shard_map/psum | solution.py:83
  645.5 0.9 rsqrt_multiply_fusion.1
  647.7 54.8 %all-reduce.37.cloned.1.call-done = f32[128,256]{1,0:T(8,128)} async-done(((f32[128,256]{1,0:T(8,128)}), f32[128,256]{1,0:T(8,128)}) %all-reduce.37.cloned.1.call-update) | async-done | bytes 131088 | tf_op jit(solution)/shard_map/psum | solution.py:84
  702.5 0.9 rsqrt_multiply_fusion
  704.8 10.7 %multiply_select_fusion = f32[1,1,48,256,256]{4,3,2,1,0:T(8,128)} fusion(f32[1,1,48,256,256]{4,3,2,1,0:T(8,128)} %bitcast.25, f32[48,256]{1,0:T(8,128)S(1)} %gather_fusion.11, f32[48,256]{1,0:T(8,128)S(1)} %gather_fusion.10, pred[48]{0:T(512)(128)(4,1)S(1)} %iota_compare_fusion.12), kind=kLoop, calls=%fused_computation.79 | loop fusion | flops 9437184 | bytes 25264176 | tf_op jit(solution)/shard_map/jit(_where)/select_n | solution.py:89
  (239 shorter events, 58.6 us)
Async XLA Ops:
  7.2 56.2 %all-reduce.45.cloned.1.call-start = ((), (), s32[]{:S(2)}) async-start(), calls=%async_computation.13 | async-start | bytes 524288 | tf_op jit(solution)/shard_map/pmax | solution.py:77
  25.5 0.7 copy-start
  25.5 0.7 copy-start.1
  26.2 75.4 %all-reduce.21.cloned.1.call-start = ((), (), s32[]{:S(2)}) async-start(), calls=%async_computation.1 | async-start | bytes 262144 | tf_op jit(solution)/shard_map/pmax | solution.py:79
  63.4 83.1 %all-reduce.19.cloned.1.call-start = ((), (), s32[]{:S(2)}) async-start(), calls=%async_computation | async-start | bytes 262144 | tf_op jit(solution)/shard_map/pmax | solution.py:78
  64.1 136.6 %all-reduce.43.cloned.1.call-start = ((), (), s32[]{:S(2)}) async-start(), calls=%async_computation.12 | async-start | bytes 524288 | tf_op jit(solution)/shard_map/pmax | solution.py:77
  147.5 99.5 %copy-start.11 = (f32[128,256]{1,0:T(8,128)S(1)}, f32[128,256]{1,0:T(8,128)}, u32[]{:S(2)}) copy-start(f32[128,256]{1,0:T(8,128)} %all-reduce.19.cloned.1.call-done) | copy-start | bytes 393220
  147.5 136.4 %copy-start.10 = (f32[128,256]{1,0:T(8,128)S(1)}, f32[128,256]{1,0:T(8,128)}, u32[]{:S(2)}) copy-start(f32[128,256]{1,0:T(8,128)} %all-reduce.21.cloned.1.call-done) | copy-start | bytes 393220
  165.0 0.7 copy-start.2
  165.1 0.7 copy-start.3
  165.8 81.3 %all-reduce.23.cloned.1.call-start = ((), (), s32[]{:S(2)}) async-start(), calls=%async_computation.2 | async-start | bytes 262144 | tf_op jit(solution)/shard_map/pmax | solution.py:78
  200.8 83.1 %all-reduce.25.cloned.1.call-start = ((), (), s32[]{:S(2)}) async-start(), calls=%async_computation.3 | async-start | bytes 262144 | tf_op jit(solution)/shard_map/pmax | solution.py:79
  201.3 136.7 %all-reduce.41.cloned.1.call-start = ((), (), s32[]{:S(2)}) async-start(), calls=%async_computation.11 | async-start | bytes 524288 | tf_op jit(solution)/shard_map/pmax | solution.py:77
  302.4 0.7 copy-start.4
  302.4 0.7 copy-start.5
  303.1 81.3 %all-reduce.27.cloned.1.call-start = ((), (), s32[]{:S(2)}) async-start(), calls=%async_computation.4 | async-start | bytes 262144 | tf_op jit(solution)/shard_map/pmax | solution.py:78
  338.0 83.4 %all-reduce.29.cloned.1.call-start = ((), (), s32[]{:S(2)}) async-start(), calls=%async_computation.5 | async-start | bytes 262144 | tf_op jit(solution)/shard_map/pmax | solution.py:79
  338.8 136.8 %all-reduce.39.cloned.1.call-start = ((), (), s32[]{:S(2)}) async-start(), calls=%async_computation.10 | async-start | bytes 524288 | tf_op jit(solution)/shard_map/pmax | solution.py:77
  439.9 0.7 copy-start.6
  439.9 0.7 copy-start.7
  440.7 81.4 %all-reduce.31.cloned.1.call-start = ((), (), s32[]{:S(2)}) async-start(), calls=%async_computation.6 | async-start | bytes 262144 | tf_op jit(solution)/shard_map/pmax | solution.py:78
  475.6 83.3 %all-reduce.33.cloned.1.call-start = ((), (), s32[]{:S(2)}) async-start(), calls=%async_computation.7 | async-start | bytes 262144 | tf_op jit(solution)/shard_map/pmax | solution.py:79
  476.2 169.3 %all-reduce.35.cloned.1.call-start = ((), (), s32[]{:S(2)}) async-start(), calls=%async_computation.8 | async-start | bytes 262144 | tf_op jit(solution)/shard_map/psum | solution.py:83
  576.0 0.7 copy-start.9
  576.0 0.7 copy-start.8
  576.7 125.8 %all-reduce.37.cloned.1.call-start = ((), (), s32[]{:S(2)}) async-start(), calls=%async_computation.9 | async-start | bytes 262144 | tf_op jit(solution)/shard_map/psum | solution.py:84
Sparse Core Ops, SparseCore 0:
  26.3 36.9 all-reduce.44
  65.7 35.8 all-reduce.20
  104.5 41.9 all-reduce.18
  165.9 34.8 all-reduce.42
  203.5 43.4 all-reduce.22
  249.2 34.6 all-reduce.24
  303.2 34.7 all-reduce.40
  340.9 43.4 all-reduce.26
  386.8 34.6 all-reduce.28
  440.8 34.7 all-reduce.38
  478.5 43.4 all-reduce.30
  524.2 34.6 all-reduce.32
  576.8 68.5 all-reduce.34
  648.2 54.2 all-reduce.36
where the time goes:
time: 724 us; the launch traced here: 722 us
  waiting for transfers between devices  593 us (82%)
  other arithmetic  88.1 us (12%)
  local copies, waits for them, and re-layouts  23.1 us (3%)
  between operations  14.9 us (2%)
    pmax x4, waiting for transfers between devices, shards(): row_peak = lax.pmax(row_pair, 'col')  181 us
    pmax x4, waiting for transfers between devices, shards(): col_peak = lax.pmax(col_pair, 'row')  145 us
    pmax x4, waiting for transfers between devices, shards(): row_pair, col_pair = lax.pmax((row_part, col_part), 'depth')  140 us
    psum x1, waiting for transfers between devices, shards(): row_mass = lax.psum(row_part, ('col', 'depth'))  68.2 us
    psum x1, waiting for transfers between devices, shards(): col_mass = lax.psum(col_part, ('row', 'depth'))  54.8 us
    reduce_max x12, other arithmetic, step_block(): magnitude.max(axis=1)[None]  28.1 us
  transfers between devices with their start and end apart: 14, of which 14 were waited for; matrix products, arithmetic and copies ran while one was open for 1% of the time, Pallas kernels for 0%

commit v1 on v0

--- a/solution.py
+++ b/solution.py
@@ -3,6 +3,7 @@
 import jax.numpy as jnp
 from jax import lax
 from jax.sharding import PartitionSpec as P
+from jax.lax import all_gather
 
 RB_DEV = 128
 ANCHORS = 16
@@ -81,7 +82,11 @@
         col_factor = col_factor * lax.rsqrt(col_peak + EPS)
     row_part, col_part = partials(row_factor, col_factor, True)
     row_mass = lax.psum(row_part, ("col", "depth"))
-    col_mass = lax.psum(col_part, ("row", "depth"))
+
+    def yards_take(matrix):
+        return jnp.sum(all_gather(matrix, ("row", "depth")), 0)
+
+    col_mass = yards_take(col_part)
     row_factor = row_factor * lax.rsqrt(row_mass + EPS)
     col_factor = col_factor * lax.rsqrt(col_mass + EPS)
     live_all = jnp.arange(slot_count, dtype=jnp.int32) < live_count

time: 724 us -> 691 us (0.954)
  waiting for transfers between devices: 593 us -> 560 us
    psum x1 -> x0, waiting for transfers between devices: 54.8 us -> none  [shards(): col_mass = lax.psum(col_part, ('row', 'depth'))]
    all_gather x0 -> x1, waiting for transfers between devices: none -> 21.4 us  [yards_take(): return jnp.sum(all_gather(matrix, ('row', 'depth')), 0)]
where the time goes in v1:
time: 691 us; the launch traced here: 689 us
  waiting for transfers between devices  560 us (81%)
  other arithmetic  88.5 us (13%)
  local copies, waits for them, and re-layouts  23.1 us (3%)
  between operations  14.9 us (2%)
    pmax x4, waiting for transfers between devices, shards(): row_peak = lax.pmax(row_pair, 'col')  181 us
    pmax x4, waiting for transfers between devices, shards(): col_peak = lax.pmax(col_pair, 'row')  145 us
    pmax x4, waiting for transfers between devices, shards(): row_pair, col_pair = lax.pmax((row_part, col_part), 'depth')  142 us
    psum x1, waiting for transfers between devices, shards(): row_mass = lax.psum(row_part, ('col', 'depth'))  66.8 us
    reduce_max x12, other arithmetic, step_block(): magnitude.max(axis=1)[None]  28.1 us
    all_gather x1, waiting for transfers between devices, yards_take(): return jnp.sum(all_gather(matrix, ('row', 'depth')), 0)  21.4 us
  transfers between devices with their start and end apart: 14, of which 14 were waited for; matrix products, arithmetic and copies ran while one was open for 1% of the time, Pallas kernels for 0%

profile of v1, /device:TPU:0, one launch (start us, length us, event | category | flops | bytes accessed | tf_op | source)
XLA Modules:
  0.0 689.1 jit_solution(12937153035157331872)
XLA Ops:
  7.9 17.5 %while.75 = (s32[]{:T(128)}, f32[128,256]{1,0:T(8,128)S(1)}, f32[128,256]{1,0:T(8,128)S(1)}, s32[]{:T(128)}, s32[48]{0:T(128)}, /*index=5*/s32[]{:T(128)}, f32[4...) while((s32[]{:T(128)}, f32[128,256]{1,0:T(8,128)S(1)}, ...), condition=%wide.region_5.6_spmd.clone.clone, body=%wide.region_0.5_spmd.clone.clone.sunk | while | flops 4194374 | bytes 3371599 | solution.py:72
  10.6 2.3 fusion.33
  14.4 0.8 compare_select_fusion.17
  16.4 2.3 fusion.33
  20.3 0.8 compare_select_fusion.17
  22.3 2.3 fusion.33
  26.2 37.1 %all-reduce.42.cloned.1.call-done = (f32[128,256]{1,0:T(8,128)}, f32[128,256]{1,0:T(8,128)}) async-done(((f32[128,256]{1,0:T(8,128)}, f32[128,256]{1,0:T(8,128)}), (f32[128,256]{1,0:T(8,128)}, f32[128,256]{1,0:T(8,128)})) %all-reduce.42.cloned.1.call-update) | async-done | bytes 262160 | tf_op jit(solution)/shard_map/pmax | solution.py:78
  64.2 37.4 %all-reduce.20.cloned.1.call-done = f32[128,256]{1,0:T(8,128)} async-done(((f32[128,256]{1,0:T(8,128)}), f32[128,256]{1,0:T(8,128)}) %all-reduce.20.cloned.1.call-update) | async-done | bytes 131088 | tf_op jit(solution)/shard_map/pmax | solution.py:80
  101.6 0.9 add_rsqrt_fusion
  102.5 44.0 %all-reduce.18.cloned.1.call-done = f32[128,256]{1,0:T(8,128)} async-done(((f32[128,256]{1,0:T(8,128)}), f32[128,256]{1,0:T(8,128)}) %all-reduce.18.cloned.1.call-update) | async-done | bytes 131088 | tf_op jit(solution)/shard_map/pmax | solution.py:79
  146.5 0.9 add_rsqrt_fusion.1
  147.5 17.5 %while.76 = (s32[]{:T(128)}, f32[128,256]{1,0:T(8,128)S(1)}, f32[128,256]{1,0:T(8,128)S(1)}, s32[]{:T(128)}, s32[48]{0:T(128)}, /*index=5*/s32[]{:T(128)}, f32[4...) while((s32[]{:T(128)}, f32[128,256]{1,0:T(8,128)S(1)}, ...), condition=%wide.region_15.16_spmd.clone.clone, body=%wide.region_10.15_spmd.clone.clone.sunk | while | flops 4194374 | bytes 3240531 | solution.py:72
  148.3 0.8 compare_select_fusion.18
  150.2 2.3 fusion.34
  156.0 2.3 fusion.34
  161.8 2.3 fusion.34
  165.8 34.9 %all-reduce.40.cloned.1.call-done = (f32[128,256]{1,0:T(8,128)}, f32[128,256]{1,0:T(8,128)}) async-done(((f32[128,256]{1,0:T(8,128)}, f32[128,256]{1,0:T(8,128)}), (f32[128,256]{1,0:T(8,128)}, f32[128,256]{1,0:T(8,128)})) %all-reduce.40.cloned.1.call-update) | async-done | bytes 262160 | tf_op jit(solution)/shard_map/pmax | solution.py:78
  201.4 45.6 %all-reduce.22.cloned.1.call-done = f32[128,256]{1,0:T(8,128)} async-done(((f32[128,256]{1,0:T(8,128)}), f32[128,256]{1,0:T(8,128)}) %all-reduce.22.cloned.1.call-update) | async-done | bytes 131088 | tf_op jit(solution)/shard_map/pmax | solution.py:79
  247.0 0.9 rsqrt_multiply_fusion.7
  248.0 35.9 %all-reduce.24.cloned.1.call-done = f32[128,256]{1,0:T(8,128)} async-done(((f32[128,256]{1,0:T(8,128)}), f32[128,256]{1,0:T(8,128)}) %all-reduce.24.cloned.1.call-update) | async-done | bytes 131088 | tf_op jit(solution)/shard_map/pmax | solution.py:80
  283.9 0.9 rsqrt_multiply_fusion.6
  284.9 17.5 %while.77 = (s32[]{:T(128)}, f32[128,256]{1,0:T(8,128)S(1)}, f32[128,256]{1,0:T(8,128)S(1)}, s32[]{:T(128)}, s32[48]{0:T(128)}, /*index=5*/s32[]{:T(128)}, f32[4...) while((s32[]{:T(128)}, f32[128,256]{1,0:T(8,128)S(1)}, ...), condition=%wide.region_25.26_spmd.clone.clone, body=%wide.region_20.25_spmd.clone.clone.sunk | while | flops 4194374 | bytes 3240531 | solution.py:72
  287.5 2.3 fusion.35
  293.3 2.3 fusion.35
  299.1 2.3 fusion.35
  303.2 34.9 %all-reduce.38.cloned.1.call-done = (f32[128,256]{1,0:T(8,128)}, f32[128,256]{1,0:T(8,128)}) async-done(((f32[128,256]{1,0:T(8,128)}, f32[128,256]{1,0:T(8,128)}), (f32[128,256]{1,0:T(8,128)}, f32[128,256]{1,0:T(8,128)})) %all-reduce.38.cloned.1.call-update) | async-done | bytes 262160 | tf_op jit(solution)/shard_map/pmax | solution.py:78
  338.8 45.6 %all-reduce.26.cloned.1.call-done = f32[128,256]{1,0:T(8,128)} async-done(((f32[128,256]{1,0:T(8,128)}), f32[128,256]{1,0:T(8,128)}) %all-reduce.26.cloned.1.call-update) | async-done | bytes 131088 | tf_op jit(solution)/shard_map/pmax | solution.py:79
  384.5 0.9 rsqrt_multiply_fusion.5
  385.4 36.1 %all-reduce.28.cloned.1.call-done = f32[128,256]{1,0:T(8,128)} async-done(((f32[128,256]{1,0:T(8,128)}), f32[128,256]{1,0:T(8,128)}) %all-reduce.28.cloned.1.call-update) | async-done | bytes 131088 | tf_op jit(solution)/shard_map/pmax | solution.py:80
  421.5 0.9 rsqrt_multiply_fusion.4
  422.5 17.5 %while.78 = (s32[]{:T(128)}, f32[128,256]{1,0:T(8,128)S(1)}, f32[128,256]{1,0:T(8,128)S(1)}, s32[]{:T(128)}, s32[48]{0:T(128)}, /*index=5*/s32[]{:T(128)}, f32[4...) while((s32[]{:T(128)}, f32[128,256]{1,0:T(8,128)S(1)}, ...), condition=%wide.region_35.36_spmd.clone.clone, body=%wide.region_30.35_spmd.clone.clone.sunk | while | flops 4194374 | bytes 3240531 | solution.py:72
  425.0 2.3 fusion.36
  430.9 2.3 fusion.36
  436.7 2.3 fusion.36
  440.7 34.9 %all-reduce.36.cloned.1.call-done = (f32[128,256]{1,0:T(8,128)}, f32[128,256]{1,0:T(8,128)}) async-done(((f32[128,256]{1,0:T(8,128)}, f32[128,256]{1,0:T(8,128)}), (f32[128,256]{1,0:T(8,128)}, f32[128,256]{1,0:T(8,128)})) %all-reduce.36.cloned.1.call-update) | async-done | bytes 262160 | tf_op jit(solution)/shard_map/pmax | solution.py:78
  476.2 45.8 %all-reduce.30.cloned.1.call-done = f32[128,256]{1,0:T(8,128)} async-done(((f32[128,256]{1,0:T(8,128)}), f32[128,256]{1,0:T(8,128)}) %all-reduce.30.cloned.1.call-update) | async-done | bytes 131088 | tf_op jit(solution)/shard_map/pmax | solution.py:79
  522.0 0.9 rsqrt_multiply_fusion.3
  522.9 35.9 %all-reduce.32.cloned.1.call-done = f32[128,256]{1,0:T(8,128)} async-done(((f32[128,256]{1,0:T(8,128)}), f32[128,256]{1,0:T(8,128)}) %all-reduce.32.cloned.1.call-update) | async-done | bytes 131088 | tf_op jit(solution)/shard_map/pmax | solution.py:80
  558.9 0.9 rsqrt_multiply_fusion.2
  559.9 16.1 %while.79 = (s32[]{:T(128)}, f32[128,256]{1,0:T(8,128)S(1)}, f32[128,256]{1,0:T(8,128)S(1)}, s32[]{:T(128)}, s32[48]{0:T(128)}, /*index=5*/s32[]{:T(128)}, f32[4...) while((s32[]{:T(128)}, f32[128,256]{1,0:T(8,128)S(1)}, ...), condition=%wide.region_43.44_spmd.clone.clone, body=%wide.region_40.43_spmd.clone.clone.sunk | while | flops 9502790 | bytes 2712147 | solution.py:72
  562.5 2.3 fusion.39
  567.8 2.3 fusion.39
  573.2 2.3 fusion.39
  578.6 66.8 %all-reduce.34.cloned.1.call-done = f32[128,256]{1,0:T(8,128)} async-done(((f32[128,256]{1,0:T(8,128)}), f32[128,256]{1,0:T(8,128)}) %all-reduce.34.cloned.1.call-update) | async-done | bytes 131088 | tf_op jit(solution)/shard_map/psum | solution.py:84
  645.5 0.9 rsqrt_multiply_fusion.1
  647.7 21.4 %all-gather.3.cloned.1.call-done = f32[1024,256]{1,0:T(8,128)} async-done(((f32[128,256]{1,0:T(8,128)}), f32[1024,256]{1,0:T(8,128)}) %all-gather.3.cloned.1.call-update) | async-done | bytes 1048592 | tf_op jit(solution)/shard_map/all_gather | solution.py:87
  669.2 1.3 reduce_sum.29
  671.8 10.7 %multiply_select_fusion = f32[1,1,48,256,256]{4,3,2,1,0:T(8,128)} fusion(f32[1,1,48,256,256]{4,3,2,1,0:T(8,128)} %bitcast.26, f32[48,256]{1,0:T(8,128)S(1)} %gather_fusion.11, f32[48,256]{1,0:T(8,128)S(1)} %gather_fusion.10, pred[48]{0:T(512)(128)(4,1)S(1)} %iota_compare_fusion.12), kind=kLoop, calls=%fused_computation.79 | loop fusion | flops 9437184 | bytes 25264176 | tf_op jit(solution)/shard_map/jit(_where)/select_n | solution.py:94
  (240 shorter events, 58.7 us)
Async XLA Ops:
  7.2 56.2 %all-reduce.42.cloned.1.call-start = ((), (), s32[]{:S(2)}) async-start(), calls=%async_computation.13 | async-start | bytes 524288 | tf_op jit(solution)/shard_map/pmax | solution.py:78
  25.5 0.7 copy-start
  25.5 0.7 copy-start.1
  26.2 75.4 %all-reduce.20.cloned.1.call-start = ((), (), s32[]{:S(2)}) async-start(), calls=%async_computation.1 | async-start | bytes 262144 | tf_op jit(solution)/shard_map/pmax | solution.py:80
  63.4 83.1 %all-reduce.18.cloned.1.call-start = ((), (), s32[]{:S(2)}) async-start(), calls=%async_computation | async-start | bytes 262144 | tf_op jit(solution)/shard_map/pmax | solution.py:79
  64.1 136.6 %all-reduce.40.cloned.1.call-start = ((), (), s32[]{:S(2)}) async-start(), calls=%async_computation.12 | async-start | bytes 524288 | tf_op jit(solution)/shard_map/pmax | solution.py:78
  147.5 99.5 %copy-start.11 = (f32[128,256]{1,0:T(8,128)S(1)}, f32[128,256]{1,0:T(8,128)}, u32[]{:S(2)}) copy-start(f32[128,256]{1,0:T(8,128)} %all-reduce.18.cloned.1.call-done) | copy-start | bytes 393220
  147.5 136.4 %copy-start.10 = (f32[128,256]{1,0:T(8,128)S(1)}, f32[128,256]{1,0:T(8,128)}, u32[]{:S(2)}) copy-start(f32[128,256]{1,0:T(8,128)} %all-reduce.20.cloned.1.call-done) | copy-start | bytes 393220
  165.0 0.7 copy-start.2
  165.1 0.7 copy-start.3
  165.8 81.3 %all-reduce.22.cloned.1.call-start = ((), (), s32[]{:S(2)}) async-start(), calls=%async_computation.2 | async-start | bytes 262144 | tf_op jit(solution)/shard_map/pmax | solution.py:79
  200.8 83.1 %all-reduce.24.cloned.1.call-start = ((), (), s32[]{:S(2)}) async-start(), calls=%async_computation.3 | async-start | bytes 262144 | tf_op jit(solution)/shard_map/pmax | solution.py:80
  201.3 136.7 %all-reduce.38.cloned.1.call-start = ((), (), s32[]{:S(2)}) async-start(), calls=%async_computation.11 | async-start | bytes 524288 | tf_op jit(solution)/shard_map/pmax | solution.py:78
  302.4 0.7 copy-start.4
  302.4 0.7 copy-start.5
  303.1 81.3 %all-reduce.26.cloned.1.call-start = ((), (), s32[]{:S(2)}) async-start(), calls=%async_computation.4 | async-start | bytes 262144 | tf_op jit(solution)/shard_map/pmax | solution.py:79
  338.0 83.4 %all-reduce.28.cloned.1.call-start = ((), (), s32[]{:S(2)}) async-start(), calls=%async_computation.5 | async-start | bytes 262144 | tf_op jit(solution)/shard_map/pmax | solution.py:80
  338.8 136.8 %all-reduce.36.cloned.1.call-start = ((), (), s32[]{:S(2)}) async-start(), calls=%async_computation.10 | async-start | bytes 524288 | tf_op jit(solution)/shard_map/pmax | solution.py:78
  439.9 0.7 copy-start.6
  439.9 0.7 copy-start.7
  440.7 81.4 %all-reduce.30.cloned.1.call-start = ((), (), s32[]{:S(2)}) async-start(), calls=%async_computation.6 | async-start | bytes 262144 | tf_op jit(solution)/shard_map/pmax | solution.py:79
  475.6 83.3 %all-reduce.32.cloned.1.call-start = ((), (), s32[]{:S(2)}) async-start(), calls=%async_computation.7 | async-start | bytes 262144 | tf_op jit(solution)/shard_map/pmax | solution.py:80
  476.2 169.3 %all-reduce.34.cloned.1.call-start = ((), (), s32[]{:S(2)}) async-start(), calls=%async_computation.8 | async-start | bytes 262144 | tf_op jit(solution)/shard_map/psum | solution.py:84
  576.0 0.7 copy-start.9
  576.0 0.7 copy-start.8
  576.7 92.5 %all-gather.3.cloned.1.call-start = ((), (), s32[]{:S(2)}) async-start(), calls=%async_computation.9 | async-start | bytes 1179648 | tf_op jit(solution)/shard_map/all_gather | solution.py:87
Sparse Core Ops, SparseCore 0:
  26.3 36.9 all-reduce.41
  65.7 35.8 all-reduce.19
  104.5 41.9 all-reduce.17
  165.9 34.8 all-reduce.39
  203.5 43.4 all-reduce.21
  249.2 34.6 all-reduce.23
  303.2 34.7 all-reduce.37
  340.9 43.4 all-reduce.25
  386.8 34.6 all-reduce.27
  440.8 34.7 all-reduce.35
  478.5 43.4 all-reduce.29
  524.2 34.6 all-reduce.31
  576.8 68.5 all-reduce.33
  647.5 21.6 all-gather.2
